TPU v7x, 32 devices: a whole 2x2x4 slice. The times are simulated.
32 devices in a mesh: gx: 4 (over x, core), gy: 8 (over z, y).
Axes of the slice: x: 2, y: 2, z: 4, core: 2. Of those that a mesh axis runs over, the one named last changes fastest.
Arguments:
- electric: float32 [3, 64, 128, 256], P(None, 'gx', 'gy'), may hold values from -6 to 6
- magnetic: float32 [3, 64, 128, 256], P(None, 'gx', 'gy'), may hold values from -6 to 6
- aux_electric: float32 [6, 64, 128, 256], P(None, 'gx', 'gy'), may hold values from -3 to 3
- aux_magnetic: float32 [6, 64, 128, 256], P(None, 'gx', 'gy'), may hold values from -3 to 3
- grades: int32 [3, 64, 128, 256], P(None, 'gx', 'gy'), may hold values from 0 to 3
- permittivity: float32 [64, 128, 256], P('gx', 'gy'), may hold values from 1 to 8
- dipole_cell: int32 [3, 16384], P(None, ('gx', 'gy')), may hold values from 0 to 255, as said below
- dipole_port: int32 [16384], P(('gx', 'gy')), may hold values from 0 to 511
- live_count: int32 [32], P(('gx', 'gy')), may hold values from 1 to 512, as said below
- injection: bfloat16 [16384, 512], P(('gx', 'gy')), may hold values from -0.25 to 0.25
- waveform: bfloat16 [512, 16], replicated, may hold values from -6 to 6
Outputs:
- electric_out: float32 [3, 64, 128, 256], P(None, 'gx', 'gy')
- magnetic_out: float32 [3, 64, 128, 256], P(None, 'gx', 'gy')
- port_power: float32 [16, 512], replicated
Inputs may be any that keep to these rules, and one draw needn't show every extreme that they name: `dipole_cell`: slot s lies in the block of cells held by the device that holds slot s. The live slots of a device are its first live_count ones; some device has all 512 live.
All inputs are finite; a program needn't handle non-finite values.
Results may differ from a plain program's by a relative error of at most 0.0003.
Values sent between devices are 32-bit elements; how exact they have to be, the bound alone decides.
A program may use at most 128 MiB of HBM per device.

v0:
```python
import jax
import jax.numpy as jnp
from jax import lax
from jax.sharding import PartitionSpec as P

courant = 0.55
absorb_keep = (0.0, 0.92, 0.75, 0.45)
absorb_take = (0.0, -0.06, -0.18, -0.35)
derivative_pairs = ((2, 1), (1, 2), (0, 2), (2, 0), (1, 0), (0, 1))


def passed_along(block, axis, distance):
    devices = range(lax.axis_size(axis))
    route = [(i - distance, i) for i in devices if i - distance in devices]
    return lax.ppermute(block, axis, route)


def difference(values, axis, plane, forward):
    length = values.shape[axis]
    if plane is None:
        shape = list(values.shape)
        shape[axis] = 1
        plane = jnp.zeros(shape, values.dtype)
    if forward:
        after = jnp.concatenate([lax.slice_in_dim(values, 1, length, axis=axis), plane], axis)
        return after - values
    before = jnp.concatenate([plane, lax.slice_in_dim(values, 0, length - 1, axis=axis)], axis)
    return values - before


def grade_table(grades, table):
    result = jnp.zeros(grades.shape, jnp.float32)
    for level in range(1, 4):
        result = result + jnp.where(grades == level, table[level], 0.0)
    return result


def curl_parts(field, auxiliary, keep, take, planes, forward):
    terms = []
    updated = []
    for number, (component, axis) in enumerate(derivative_pairs):
        plane = None
        if planes is not None and axis == 0:
            plane = planes[0][component - 1]
        if planes is not None and axis == 1:
            plane = planes[1][component // 2]
        slope = difference(field[component], axis, plane, forward)
        carried = keep[axis] * auxiliary[number] + take[axis] * slope
        terms.append(slope + carried)
        updated.append(carried)
    rotation = (terms[0] - terms[1], terms[2] - terms[3], terms[4] - terms[5])
    return (rotation, tuple(updated))


def inject(z_plane, current_now, cell_table, depth_table):
    weighted = cell_table * current_now[:, None]
    source = lax.dot_general(
        weighted, depth_table, (((0,), (0,)), ((), ())), precision=lax.Precision.HIGHEST
    )
    return z_plane - courant * source.reshape(z_plane.shape)


def read_cells(z_plane, cell_table, depth_table):
    rows = z_plane.reshape(cell_table.shape[1], depth_table.shape[1])
    picked = jnp.dot(cell_table, rows, precision=lax.Precision.HIGHEST)
    return jnp.sum(picked * depth_table, axis=1)


def note_power(record, drive, index):
    return lax.dynamic_update_slice_in_dim(record, drive[None, :], index, 0)


def local(
    electric,
    magnetic,
    aux_electric,
    aux_magnetic,
    grades,
    permittivity,
    dipole_cell,
    dipole_port,
    live_count,
    injection,
    waveform,
):
    depth_x, depth_y, depth_z = electric.shape[1:]
    slots = dipole_cell.shape[1]
    ports, steps = waveform.shape
    row_index = lax.axis_index("gx")
    col_index = lax.axis_index("gy")
    plane_cell = (dipole_cell[0] - row_index * depth_x) * depth_y + (
        dipole_cell[1] - col_index * depth_y
    )
    cell_table = (
        plane_cell[:, None] == jnp.arange(depth_x * depth_y, dtype=jnp.int32)[None, :]
    ).astype(jnp.float32)
    depth_table = (dipole_cell[2][:, None] == jnp.arange(depth_z, dtype=jnp.int32)[None, :]).astype(
        jnp.float32
    )
    live = (jnp.arange(slots, dtype=jnp.int32) < live_count[0]).astype(jnp.float32)
    current = jnp.dot(injection, waveform, preferred_element_type=jnp.float32) * live[:, None]
    members = (dipole_port[:, None] == jnp.arange(ports, dtype=jnp.int32)[None, :]).astype(
        jnp.float32
    )
    factor = courant / permittivity
    keep = grade_table(grades, absorb_keep)
    take = grade_table(grades, absorb_take)
    record = jnp.zeros((steps, slots), jnp.float32)

    def turn_parts(step, carry):
        field_e, field_h, memory_e, memory_h, record = carry
        next_x = passed_along(jnp.stack([field_e[1][0:1], field_e[2][0:1]]), "gx", -1)
        next_y = passed_along(jnp.stack([field_e[0][:, 0:1], field_e[2][:, 0:1]]), "gy", -1)
        rotation, memory_e = curl_parts(field_e, memory_e, keep, take, (next_x, next_y), True)
        field_h = tuple((field_h[number] - courant * rotation[number] for number in range(3)))
        prior_x = passed_along(jnp.stack([field_h[1][-1:], field_h[2][-1:]]), "gx", 1)
        prior_y = passed_along(jnp.stack([field_h[0][:, -1:], field_h[2][:, -1:]]), "gy", 1)
        rotation, memory_h = curl_parts(field_h, memory_h, keep, take, (prior_x, prior_y), False)
        current_now = lax.dynamic_slice_in_dim(current, step, 1, 1)[:, 0]
        z_plane = inject(field_e[2] + factor * rotation[2], current_now, cell_table, depth_table)
        field_e = (field_e[0] + factor * rotation[0], field_e[1] + factor * rotation[1], z_plane)
        drive = current_now * read_cells(z_plane, cell_table, depth_table)
        record = note_power(record, drive, step)
        return (field_e, field_h, memory_e, memory_h, record)

    start_state = (
        tuple((electric[number] for number in range(3))),
        tuple((magnetic[number] for number in range(3))),
        tuple((aux_electric[number] for number in range(6))),
        tuple((aux_magnetic[number] for number in range(6))),
        record,
    )
    parts_e, parts_h, parts_me, parts_mh, record = lax.fori_loop(0, steps, turn_parts, start_state)
    electric = jnp.stack(parts_e)
    magnetic = jnp.stack(parts_h)
    partial_value = jnp.dot(record, members, precision=lax.Precision.HIGHEST)
    port_power = lax.psum(partial_value, ("gx", "gy"))
    return (electric, magnetic, port_power)


def solution(mesh):
    in_specs = (
        P(None, "gx", "gy", None),
        P(None, "gx", "gy", None),
        P(None, "gx", "gy", None),
        P(None, "gx", "gy", None),
        P(None, "gx", "gy", None),
        P("gx", "gy", None),
        P(None, ("gx", "gy")),
        P(("gx", "gy")),
        P(("gx", "gy")),
        P(("gx", "gy"), None),
        P(),
    )
    out_specs = (P(None, "gx", "gy", None), P(None, "gx", "gy", None), P())
    return jax.shard_map(local, mesh=mesh, in_specs=in_specs, out_specs=out_specs, check_vma=False)
```

profile of v0, /device:TPU:0, one launch (start us, length us, event | category | flops | bytes accessed | tf_op | source)
XLA Modules:
  0.0 605.0 jit_solution(2541762445763992828)
XLA Ops:
  10.5 545.4 %while.50 = (s32[]{:T(128)}, f32[16,16,256]{2,1,0:T(8,128)S(1)}, f32[16,16,256]{2,1,0:T(8,128)S(1)}, f32[16,16,256]{2,1,0:T(8,128)S(1)}, f32[16,16,256]{2,1,0:T(...) while((s32[]{:T(128)}, f32[16,16,256]{2,1,0:T(8,128)S(1)}, ...), condition=%wide.region_2.3_spmd.clone, body=%wide.region_0.2_spmd.clone.sunk | while | flops 812285952 | bytes 56044672 | solution.py:133
  20.5 2.4 multiply_subtract_fusion.7
  23.5 5.5 collective-permute-start.2
  30.9 2.8 collective-permute-start.3
  52.6 2.4 multiply_subtract_fusion.7
  55.6 5.4 collective-permute-start.2
  63.0 3.8 collective-permute-start.3
  85.7 2.4 multiply_subtract_fusion.7
  88.7 5.2 collective-permute-start.2
  95.8 5.3 collective-permute-start.3
  120.0 2.4 multiply_subtract_fusion.7
  123.0 5.2 collective-permute-start.2
  130.1 5.3 collective-permute-start.3
  154.3 2.4 multiply_subtract_fusion.7
  157.3 5.2 collective-permute-start.2
  164.4 5.3 collective-permute-start.3
  188.6 2.4 multiply_subtract_fusion.7
  191.6 5.2 collective-permute-start.2
  198.7 5.3 collective-permute-start.3
  222.9 2.4 multiply_subtract_fusion.7
  225.9 5.2 collective-permute-start.2
  233.0 5.3 collective-permute-start.3
  257.2 2.4 multiply_subtract_fusion.7
  260.2 5.2 collective-permute-start.2
  267.3 5.3 collective-permute-start.3
  291.5 2.4 multiply_subtract_fusion.7
  294.5 5.2 collective-permute-start.2
  301.6 5.3 collective-permute-start.3
  325.8 2.4 multiply_subtract_fusion.7
  328.8 5.2 collective-permute-start.2
  335.9 5.3 collective-permute-start.3
  360.1 2.4 multiply_subtract_fusion.7
  363.1 5.2 collective-permute-start.2
  370.2 5.3 collective-permute-start.3
  394.4 2.4 multiply_subtract_fusion.7
  397.4 5.2 collective-permute-start.2
  404.5 5.3 collective-permute-start.3
  428.7 2.4 multiply_subtract_fusion.7
  431.7 5.2 collective-permute-start.2
  438.8 5.3 collective-permute-start.3
  463.0 2.4 multiply_subtract_fusion.7
  466.0 5.2 collective-permute-start.2
  473.1 5.3 collective-permute-start.3
  500.3 5.2 collective-permute-start.2
  507.4 5.3 collective-permute-start.3
  534.6 5.2 collective-permute-start.2
  541.7 5.3 collective-permute-start.3
  557.2 45.9 %psum.7 = f32[16,512]{1,0:T(8,128)} all-reduce(f32[16,512]{1,0:T(8,128)S(1)} %fusion.27), channel_id=1, replica_groups=mesh['gx'=4,'gy'=8] {'gx','gy'}, use_global_device_ids=true, to_apply=%region_3.4 | all-reduce | flops 8192 | bytes 65536 | tf_op jit(solution)/shard_map/psum | solution.py:137
  (1470 shorter events, 352.0 us)
Async XLA Ops:
  10.6 9.9 %collective-permute-start.1 = (f32[2,16,1,256]{3,2,1,0:T(1,128)S(1)}, f32[2,16,1,256]{3,2,1,0:T(1,128)S(1)}, u32[]{:S(2)}, u32[]{:S(2)}) collective-permute-start(f32[2,16,1,256]{3,2,1,0:T(1,128)S(1)} %pad_maximum_fusion.11), channel_id=1, source_target_pairs={{1,0},{2,1},{3,2},{4,3},{5,4},{6,5},{7,6},{9,8},{10,9},{11,10},{12... | collective-permute-start | bytes 98312 | tf_op jit(solution)/shard_map/while/body/eval_jaxpr/ppermute | solution.py:15
  11.9 8.5 %collective-permute-start = (f32[2,1,16,256]{3,2,1,0:T(8,128)S(1)}, f32[2,1,16,256]{3,2,1,0:T(8,128)S(1)}, u32[]{:S(2)}, u32[]{:S(2)}) collective-permute-start(f32[2,1,16,256]{3,2,1,0:T(8,128)S(1)} %pad_maximum_fusion.10), channel_id=1, source_target_pairs={{8,0},{16,8},{24,16},{9,1},{17,9},{25,17},{10,2},{18,10},{26,18},{... | collective-permute-start | bytes 98312 | tf_op jit(solution)/shard_map/while/body/eval_jaxpr/ppermute | solution.py:15
  23.5 10.2 %collective-permute-start.2 = (f32[2,16,1,256]{3,2,1,0:T(1,128)S(1)}, f32[2,16,1,256]{3,2,1,0:T(1,128)S(1)}, u32[]{:S(2)}, u32[]{:S(2)}) collective-permute-start(f32[2,16,1,256]{3,2,1,0:T(1,128)S(1)} %pad_maximum_fusion.12), channel_id=1, source_target_pairs={{0,1},{1,2},{2,3},{3,4},{4,5},{5,6},{6,7},{8,9},{9,10},{10,11},{11... | collective-permute-start | bytes 98312 | tf_op jit(solution)/shard_map/while/body/eval_jaxpr/ppermute | solution.py:15
  42.7 9.9 %collective-permute-start.1 = (f32[2,16,1,256]{3,2,1,0:T(1,128)S(1)}, f32[2,16,1,256]{3,2,1,0:T(1,128)S(1)}, u32[]{:S(2)}, u32[]{:S(2)}) collective-permute-start(f32[2,16,1,256]{3,2,1,0:T(1,128)S(1)} %pad_maximum_fusion.11), channel_id=1, source_target_pairs={{1,0},{2,1},{3,2},{4,3},{5,4},{6,5},{7,6},{9,8},{10,9},{11,10},{12... | collective-permute-start | bytes 98312 | tf_op jit(solution)/shard_map/while/body/eval_jaxpr/ppermute | solution.py:15
  44.0 8.5 %collective-permute-start = (f32[2,1,16,256]{3,2,1,0:T(8,128)S(1)}, f32[2,1,16,256]{3,2,1,0:T(8,128)S(1)}, u32[]{:S(2)}, u32[]{:S(2)}) collective-permute-start(f32[2,1,16,256]{3,2,1,0:T(8,128)S(1)} %pad_maximum_fusion.10), channel_id=1, source_target_pairs={{8,0},{16,8},{24,16},{9,1},{17,9},{25,17},{10,2},{18,10},{26,18},{... | collective-permute-start | bytes 98312 | tf_op jit(solution)/shard_map/while/body/eval_jaxpr/ppermute | solution.py:15
  55.6 11.2 %collective-permute-start.2 = (f32[2,16,1,256]{3,2,1,0:T(1,128)S(1)}, f32[2,16,1,256]{3,2,1,0:T(1,128)S(1)}, u32[]{:S(2)}, u32[]{:S(2)}) collective-permute-start(f32[2,16,1,256]{3,2,1,0:T(1,128)S(1)} %pad_maximum_fusion.12), channel_id=1, source_target_pairs={{0,1},{1,2},{2,3},{3,4},{4,5},{5,6},{6,7},{8,9},{9,10},{10,11},{11... | collective-permute-start | bytes 98312 | tf_op jit(solution)/shard_map/while/body/eval_jaxpr/ppermute | solution.py:15
  75.8 9.9 %collective-permute-start.1 = (f32[2,16,1,256]{3,2,1,0:T(1,128)S(1)}, f32[2,16,1,256]{3,2,1,0:T(1,128)S(1)}, u32[]{:S(2)}, u32[]{:S(2)}) collective-permute-start(f32[2,16,1,256]{3,2,1,0:T(1,128)S(1)} %pad_maximum_fusion.11), channel_id=1, source_target_pairs={{1,0},{2,1},{3,2},{4,3},{5,4},{6,5},{7,6},{9,8},{10,9},{11,10},{12... | collective-permute-start | bytes 98312 | tf_op jit(solution)/shard_map/while/body/eval_jaxpr/ppermute | solution.py:15
  77.1 8.5 %collective-permute-start = (f32[2,1,16,256]{3,2,1,0:T(8,128)S(1)}, f32[2,1,16,256]{3,2,1,0:T(8,128)S(1)}, u32[]{:S(2)}, u32[]{:S(2)}) collective-permute-start(f32[2,1,16,256]{3,2,1,0:T(8,128)S(1)} %pad_maximum_fusion.10), channel_id=1, source_target_pairs={{8,0},{16,8},{24,16},{9,1},{17,9},{25,17},{10,2},{18,10},{26,18},{... | collective-permute-start | bytes 98312 | tf_op jit(solution)/shard_map/while/body/eval_jaxpr/ppermute | solution.py:15
  88.7 12.4 %collective-permute-start.2 = (f32[2,16,1,256]{3,2,1,0:T(1,128)S(1)}, f32[2,16,1,256]{3,2,1,0:T(1,128)S(1)}, u32[]{:S(2)}, u32[]{:S(2)}) collective-permute-start(f32[2,16,1,256]{3,2,1,0:T(1,128)S(1)} %pad_maximum_fusion.12), channel_id=1, source_target_pairs={{0,1},{1,2},{2,3},{3,4},{4,5},{5,6},{6,7},{8,9},{9,10},{10,11},{11... | collective-permute-start | bytes 98312 | tf_op jit(solution)/shard_map/while/body/eval_jaxpr/ppermute | solution.py:15
  110.1 9.9 %collective-permute-start.1 = (f32[2,16,1,256]{3,2,1,0:T(1,128)S(1)}, f32[2,16,1,256]{3,2,1,0:T(1,128)S(1)}, u32[]{:S(2)}, u32[]{:S(2)}) collective-permute-start(f32[2,16,1,256]{3,2,1,0:T(1,128)S(1)} %pad_maximum_fusion.11), channel_id=1, source_target_pairs={{1,0},{2,1},{3,2},{4,3},{5,4},{6,5},{7,6},{9,8},{10,9},{11,10},{12... | collective-permute-start | bytes 98312 | tf_op jit(solution)/shard_map/while/body/eval_jaxpr/ppermute | solution.py:15
  111.4 8.5 %collective-permute-start = (f32[2,1,16,256]{3,2,1,0:T(8,128)S(1)}, f32[2,1,16,256]{3,2,1,0:T(8,128)S(1)}, u32[]{:S(2)}, u32[]{:S(2)}) collective-permute-start(f32[2,1,16,256]{3,2,1,0:T(8,128)S(1)} %pad_maximum_fusion.10), channel_id=1, source_target_pairs={{8,0},{16,8},{24,16},{9,1},{17,9},{25,17},{10,2},{18,10},{26,18},{... | collective-permute-start | bytes 98312 | tf_op jit(solution)/shard_map/while/body/eval_jaxpr/ppermute | solution.py:15
  123.0 12.4 %collective-permute-start.2 = (f32[2,16,1,256]{3,2,1,0:T(1,128)S(1)}, f32[2,16,1,256]{3,2,1,0:T(1,128)S(1)}, u32[]{:S(2)}, u32[]{:S(2)}) collective-permute-start(f32[2,16,1,256]{3,2,1,0:T(1,128)S(1)} %pad_maximum_fusion.12), channel_id=1, source_target_pairs={{0,1},{1,2},{2,3},{3,4},{4,5},{5,6},{6,7},{8,9},{9,10},{10,11},{11... | collective-permute-start | bytes 98312 | tf_op jit(solution)/shard_map/while/body/eval_jaxpr/ppermute | solution.py:15
  144.4 9.9 %collective-permute-start.1 = (f32[2,16,1,256]{3,2,1,0:T(1,128)S(1)}, f32[2,16,1,256]{3,2,1,0:T(1,128)S(1)}, u32[]{:S(2)}, u32[]{:S(2)}) collective-permute-start(f32[2,16,1,256]{3,2,1,0:T(1,128)S(1)} %pad_maximum_fusion.11), channel_id=1, source_target_pairs={{1,0},{2,1},{3,2},{4,3},{5,4},{6,5},{7,6},{9,8},{10,9},{11,10},{12... | collective-permute-start | bytes 98312 | tf_op jit(solution)/shard_map/while/body/eval_jaxpr/ppermute | solution.py:15
  145.7 8.5 %collective-permute-start = (f32[2,1,16,256]{3,2,1,0:T(8,128)S(1)}, f32[2,1,16,256]{3,2,1,0:T(8,128)S(1)}, u32[]{:S(2)}, u32[]{:S(2)}) collective-permute-start(f32[2,1,16,256]{3,2,1,0:T(8,128)S(1)} %pad_maximum_fusion.10), channel_id=1, source_target_pairs={{8,0},{16,8},{24,16},{9,1},{17,9},{25,17},{10,2},{18,10},{26,18},{... | collective-permute-start | bytes 98312 | tf_op jit(solution)/shard_map/while/body/eval_jaxpr/ppermute | solution.py:15
  157.3 12.4 %collective-permute-start.2 = (f32[2,16,1,256]{3,2,1,0:T(1,128)S(1)}, f32[2,16,1,256]{3,2,1,0:T(1,128)S(1)}, u32[]{:S(2)}, u32[]{:S(2)}) collective-permute-start(f32[2,16,1,256]{3,2,1,0:T(1,128)S(1)} %pad_maximum_fusion.12), channel_id=1, source_target_pairs={{0,1},{1,2},{2,3},{3,4},{4,5},{5,6},{6,7},{8,9},{9,10},{10,11},{11... | collective-permute-start | bytes 98312 | tf_op jit(solution)/shard_map/while/body/eval_jaxpr/ppermute | solution.py:15
  178.7 9.9 %collective-permute-start.1 = (f32[2,16,1,256]{3,2,1,0:T(1,128)S(1)}, f32[2,16,1,256]{3,2,1,0:T(1,128)S(1)}, u32[]{:S(2)}, u32[]{:S(2)}) collective-permute-start(f32[2,16,1,256]{3,2,1,0:T(1,128)S(1)} %pad_maximum_fusion.11), channel_id=1, source_target_pairs={{1,0},{2,1},{3,2},{4,3},{5,4},{6,5},{7,6},{9,8},{10,9},{11,10},{12... | collective-permute-start | bytes 98312 | tf_op jit(solution)/shard_map/while/body/eval_jaxpr/ppermute | solution.py:15
  180.0 8.5 %collective-permute-start = (f32[2,1,16,256]{3,2,1,0:T(8,128)S(1)}, f32[2,1,16,256]{3,2,1,0:T(8,128)S(1)}, u32[]{:S(2)}, u32[]{:S(2)}) collective-permute-start(f32[2,1,16,256]{3,2,1,0:T(8,128)S(1)} %pad_maximum_fusion.10), channel_id=1, source_target_pairs={{8,0},{16,8},{24,16},{9,1},{17,9},{25,17},{10,2},{18,10},{26,18},{... | collective-permute-start | bytes 98312 | tf_op jit(solution)/shard_map/while/body/eval_jaxpr/ppermute | solution.py:15
  191.6 12.4 %collective-permute-start.2 = (f32[2,16,1,256]{3,2,1,0:T(1,128)S(1)}, f32[2,16,1,256]{3,2,1,0:T(1,128)S(1)}, u32[]{:S(2)}, u32[]{:S(2)}) collective-permute-start(f32[2,16,1,256]{3,2,1,0:T(1,128)S(1)} %pad_maximum_fusion.12), channel_id=1, source_target_pairs={{0,1},{1,2},{2,3},{3,4},{4,5},{5,6},{6,7},{8,9},{9,10},{10,11},{11... | collective-permute-start | bytes 98312 | tf_op jit(solution)/shard_map/while/body/eval_jaxpr/ppermute | solution.py:15
  213.0 9.9 %collective-permute-start.1 = (f32[2,16,1,256]{3,2,1,0:T(1,128)S(1)}, f32[2,16,1,256]{3,2,1,0:T(1,128)S(1)}, u32[]{:S(2)}, u32[]{:S(2)}) collective-permute-start(f32[2,16,1,256]{3,2,1,0:T(1,128)S(1)} %pad_maximum_fusion.11), channel_id=1, source_target_pairs={{1,0},{2,1},{3,2},{4,3},{5,4},{6,5},{7,6},{9,8},{10,9},{11,10},{12... | collective-permute-start | bytes 98312 | tf_op jit(solution)/shard_map/while/body/eval_jaxpr/ppermute | solution.py:15
  214.3 8.5 %collective-permute-start = (f32[2,1,16,256]{3,2,1,0:T(8,128)S(1)}, f32[2,1,16,256]{3,2,1,0:T(8,128)S(1)}, u32[]{:S(2)}, u32[]{:S(2)}) collective-permute-start(f32[2,1,16,256]{3,2,1,0:T(8,128)S(1)} %pad_maximum_fusion.10), channel_id=1, source_target_pairs={{8,0},{16,8},{24,16},{9,1},{17,9},{25,17},{10,2},{18,10},{26,18},{... | collective-permute-start | bytes 98312 | tf_op jit(solution)/shard_map/while/body/eval_jaxpr/ppermute | solution.py:15
  225.9 12.4 %collective-permute-start.2 = (f32[2,16,1,256]{3,2,1,0:T(1,128)S(1)}, f32[2,16,1,256]{3,2,1,0:T(1,128)S(1)}, u32[]{:S(2)}, u32[]{:S(2)}) collective-permute-start(f32[2,16,1,256]{3,2,1,0:T(1,128)S(1)} %pad_maximum_fusion.12), channel_id=1, source_target_pairs={{0,1},{1,2},{2,3},{3,4},{4,5},{5,6},{6,7},{8,9},{9,10},{10,11},{11... | collective-permute-start | bytes 98312 | tf_op jit(solution)/shard_map/while/body/eval_jaxpr/ppermute | solution.py:15
  247.3 9.9 %collective-permute-start.1 = (f32[2,16,1,256]{3,2,1,0:T(1,128)S(1)}, f32[2,16,1,256]{3,2,1,0:T(1,128)S(1)}, u32[]{:S(2)}, u32[]{:S(2)}) collective-permute-start(f32[2,16,1,256]{3,2,1,0:T(1,128)S(1)} %pad_maximum_fusion.11), channel_id=1, source_target_pairs={{1,0},{2,1},{3,2},{4,3},{5,4},{6,5},{7,6},{9,8},{10,9},{11,10},{12... | collective-permute-start | bytes 98312 | tf_op jit(solution)/shard_map/while/body/eval_jaxpr/ppermute | solution.py:15
  248.6 8.5 %collective-permute-start = (f32[2,1,16,256]{3,2,1,0:T(8,128)S(1)}, f32[2,1,16,256]{3,2,1,0:T(8,128)S(1)}, u32[]{:S(2)}, u32[]{:S(2)}) collective-permute-start(f32[2,1,16,256]{3,2,1,0:T(8,128)S(1)} %pad_maximum_fusion.10), channel_id=1, source_target_pairs={{8,0},{16,8},{24,16},{9,1},{17,9},{25,17},{10,2},{18,10},{26,18},{... | collective-permute-start | bytes 98312 | tf_op jit(solution)/shard_map/while/body/eval_jaxpr/ppermute | solution.py:15
  260.2 12.4 %collective-permute-start.2 = (f32[2,16,1,256]{3,2,1,0:T(1,128)S(1)}, f32[2,16,1,256]{3,2,1,0:T(1,128)S(1)}, u32[]{:S(2)}, u32[]{:S(2)}) collective-permute-start(f32[2,16,1,256]{3,2,1,0:T(1,128)S(1)} %pad_maximum_fusion.12), channel_id=1, source_target_pairs={{0,1},{1,2},{2,3},{3,4},{4,5},{5,6},{6,7},{8,9},{9,10},{10,11},{11... | collective-permute-start | bytes 98312 | tf_op jit(solution)/shard_map/while/body/eval_jaxpr/ppermute | solution.py:15
  281.6 9.9 %collective-permute-start.1 = (f32[2,16,1,256]{3,2,1,0:T(1,128)S(1)}, f32[2,16,1,256]{3,2,1,0:T(1,128)S(1)}, u32[]{:S(2)}, u32[]{:S(2)}) collective-permute-start(f32[2,16,1,256]{3,2,1,0:T(1,128)S(1)} %pad_maximum_fusion.11), channel_id=1, source_target_pairs={{1,0},{2,1},{3,2},{4,3},{5,4},{6,5},{7,6},{9,8},{10,9},{11,10},{12... | collective-permute-start | bytes 98312 | tf_op jit(solution)/shard_map/while/body/eval_jaxpr/ppermute | solution.py:15
  282.9 8.5 %collective-permute-start = (f32[2,1,16,256]{3,2,1,0:T(8,128)S(1)}, f32[2,1,16,256]{3,2,1,0:T(8,128)S(1)}, u32[]{:S(2)}, u32[]{:S(2)}) collective-permute-start(f32[2,1,16,256]{3,2,1,0:T(8,128)S(1)} %pad_maximum_fusion.10), channel_id=1, source_target_pairs={{8,0},{16,8},{24,16},{9,1},{17,9},{25,17},{10,2},{18,10},{26,18},{... | collective-permute-start | bytes 98312 | tf_op jit(solution)/shard_map/while/body/eval_jaxpr/ppermute | solution.py:15
  294.5 12.4 %collective-permute-start.2 = (f32[2,16,1,256]{3,2,1,0:T(1,128)S(1)}, f32[2,16,1,256]{3,2,1,0:T(1,128)S(1)}, u32[]{:S(2)}, u32[]{:S(2)}) collective-permute-start(f32[2,16,1,256]{3,2,1,0:T(1,128)S(1)} %pad_maximum_fusion.12), channel_id=1, source_target_pairs={{0,1},{1,2},{2,3},{3,4},{4,5},{5,6},{6,7},{8,9},{9,10},{10,11},{11... | collective-permute-start | bytes 98312 | tf_op jit(solution)/shard_map/while/body/eval_jaxpr/ppermute | solution.py:15
  315.9 9.9 %collective-permute-start.1 = (f32[2,16,1,256]{3,2,1,0:T(1,128)S(1)}, f32[2,16,1,256]{3,2,1,0:T(1,128)S(1)}, u32[]{:S(2)}, u32[]{:S(2)}) collective-permute-start(f32[2,16,1,256]{3,2,1,0:T(1,128)S(1)} %pad_maximum_fusion.11), channel_id=1, source_target_pairs={{1,0},{2,1},{3,2},{4,3},{5,4},{6,5},{7,6},{9,8},{10,9},{11,10},{12... | collective-permute-start | bytes 98312 | tf_op jit(solution)/shard_map/while/body/eval_jaxpr/ppermute | solution.py:15
  317.2 8.5 %collective-permute-start = (f32[2,1,16,256]{3,2,1,0:T(8,128)S(1)}, f32[2,1,16,256]{3,2,1,0:T(8,128)S(1)}, u32[]{:S(2)}, u32[]{:S(2)}) collective-permute-start(f32[2,1,16,256]{3,2,1,0:T(8,128)S(1)} %pad_maximum_fusion.10), channel_id=1, source_target_pairs={{8,0},{16,8},{24,16},{9,1},{17,9},{25,17},{10,2},{18,10},{26,18},{... | collective-permute-start | bytes 98312 | tf_op jit(solution)/shard_map/while/body/eval_jaxpr/ppermute | solution.py:15
  328.8 12.4 %collective-permute-start.2 = (f32[2,16,1,256]{3,2,1,0:T(1,128)S(1)}, f32[2,16,1,256]{3,2,1,0:T(1,128)S(1)}, u32[]{:S(2)}, u32[]{:S(2)}) collective-permute-start(f32[2,16,1,256]{3,2,1,0:T(1,128)S(1)} %pad_maximum_fusion.12), channel_id=1, source_target_pairs={{0,1},{1,2},{2,3},{3,4},{4,5},{5,6},{6,7},{8,9},{9,10},{10,11},{11... | collective-permute-start | bytes 98312 | tf_op jit(solution)/shard_map/while/body/eval_jaxpr/ppermute | solution.py:15
  350.2 9.9 %collective-permute-start.1 = (f32[2,16,1,256]{3,2,1,0:T(1,128)S(1)}, f32[2,16,1,256]{3,2,1,0:T(1,128)S(1)}, u32[]{:S(2)}, u32[]{:S(2)}) collective-permute-start(f32[2,16,1,256]{3,2,1,0:T(1,128)S(1)} %pad_maximum_fusion.11), channel_id=1, source_target_pairs={{1,0},{2,1},{3,2},{4,3},{5,4},{6,5},{7,6},{9,8},{10,9},{11,10},{12... | collective-permute-start | bytes 98312 | tf_op jit(solution)/shard_map/while/body/eval_jaxpr/ppermute | solution.py:15
  351.5 8.5 %collective-permute-start = (f32[2,1,16,256]{3,2,1,0:T(8,128)S(1)}, f32[2,1,16,256]{3,2,1,0:T(8,128)S(1)}, u32[]{:S(2)}, u32[]{:S(2)}) collective-permute-start(f32[2,1,16,256]{3,2,1,0:T(8,128)S(1)} %pad_maximum_fusion.10), channel_id=1, source_target_pairs={{8,0},{16,8},{24,16},{9,1},{17,9},{25,17},{10,2},{18,10},{26,18},{... | collective-permute-start | bytes 98312 | tf_op jit(solution)/shard_map/while/body/eval_jaxpr/ppermute | solution.py:15
  363.1 12.4 %collective-permute-start.2 = (f32[2,16,1,256]{3,2,1,0:T(1,128)S(1)}, f32[2,16,1,256]{3,2,1,0:T(1,128)S(1)}, u32[]{:S(2)}, u32[]{:S(2)}) collective-permute-start(f32[2,16,1,256]{3,2,1,0:T(1,128)S(1)} %pad_maximum_fusion.12), channel_id=1, source_target_pairs={{0,1},{1,2},{2,3},{3,4},{4,5},{5,6},{6,7},{8,9},{9,10},{10,11},{11... | collective-permute-start | bytes 98312 | tf_op jit(solution)/shard_map/while/body/eval_jaxpr/ppermute | solution.py:15
  384.5 9.9 %collective-permute-start.1 = (f32[2,16,1,256]{3,2,1,0:T(1,128)S(1)}, f32[2,16,1,256]{3,2,1,0:T(1,128)S(1)}, u32[]{:S(2)}, u32[]{:S(2)}) collective-permute-start(f32[2,16,1,256]{3,2,1,0:T(1,128)S(1)} %pad_maximum_fusion.11), channel_id=1, source_target_pairs={{1,0},{2,1},{3,2},{4,3},{5,4},{6,5},{7,6},{9,8},{10,9},{11,10},{12... | collective-permute-start | bytes 98312 | tf_op jit(solution)/shard_map/while/body/eval_jaxpr/ppermute | solution.py:15
  385.8 8.5 %collective-permute-start = (f32[2,1,16,256]{3,2,1,0:T(8,128)S(1)}, f32[2,1,16,256]{3,2,1,0:T(8,128)S(1)}, u32[]{:S(2)}, u32[]{:S(2)}) collective-permute-start(f32[2,1,16,256]{3,2,1,0:T(8,128)S(1)} %pad_maximum_fusion.10), channel_id=1, source_target_pairs={{8,0},{16,8},{24,16},{9,1},{17,9},{25,17},{10,2},{18,10},{26,18},{... | collective-permute-start | bytes 98312 | tf_op jit(solution)/shard_map/while/body/eval_jaxpr/ppermute | solution.py:15
  397.4 12.4 %collective-permute-start.2 = (f32[2,16,1,256]{3,2,1,0:T(1,128)S(1)}, f32[2,16,1,256]{3,2,1,0:T(1,128)S(1)}, u32[]{:S(2)}, u32[]{:S(2)}) collective-permute-start(f32[2,16,1,256]{3,2,1,0:T(1,128)S(1)} %pad_maximum_fusion.12), channel_id=1, source_target_pairs={{0,1},{1,2},{2,3},{3,4},{4,5},{5,6},{6,7},{8,9},{9,10},{10,11},{11... | collective-permute-start | bytes 98312 | tf_op jit(solution)/shard_map/while/body/eval_jaxpr/ppermute | solution.py:15
  418.8 9.9 %collective-permute-start.1 = (f32[2,16,1,256]{3,2,1,0:T(1,128)S(1)}, f32[2,16,1,256]{3,2,1,0:T(1,128)S(1)}, u32[]{:S(2)}, u32[]{:S(2)}) collective-permute-start(f32[2,16,1,256]{3,2,1,0:T(1,128)S(1)} %pad_maximum_fusion.11), channel_id=1, source_target_pairs={{1,0},{2,1},{3,2},{4,3},{5,4},{6,5},{7,6},{9,8},{10,9},{11,10},{12... | collective-permute-start | bytes 98312 | tf_op jit(solution)/shard_map/while/body/eval_jaxpr/ppermute | solution.py:15
  420.1 8.5 %collective-permute-start = (f32[2,1,16,256]{3,2,1,0:T(8,128)S(1)}, f32[2,1,16,256]{3,2,1,0:T(8,128)S(1)}, u32[]{:S(2)}, u32[]{:S(2)}) collective-permute-start(f32[2,1,16,256]{3,2,1,0:T(8,128)S(1)} %pad_maximum_fusion.10), channel_id=1, source_target_pairs={{8,0},{16,8},{24,16},{9,1},{17,9},{25,17},{10,2},{18,10},{26,18},{... | collective-permute-start | bytes 98312 | tf_op jit(solution)/shard_map/while/body/eval_jaxpr/ppermute | solution.py:15
  431.7 12.4 %collective-permute-start.2 = (f32[2,16,1,256]{3,2,1,0:T(1,128)S(1)}, f32[2,16,1,256]{3,2,1,0:T(1,128)S(1)}, u32[]{:S(2)}, u32[]{:S(2)}) collective-permute-start(f32[2,16,1,256]{3,2,1,0:T(1,128)S(1)} %pad_maximum_fusion.12), channel_id=1, source_target_pairs={{0,1},{1,2},{2,3},{3,4},{4,5},{5,6},{6,7},{8,9},{9,10},{10,11},{11... | collective-permute-start | bytes 98312 | tf_op jit(solution)/shard_map/while/body/eval_jaxpr/ppermute | solution.py:15
  453.1 9.9 %collective-permute-start.1 = (f32[2,16,1,256]{3,2,1,0:T(1,128)S(1)}, f32[2,16,1,256]{3,2,1,0:T(1,128)S(1)}, u32[]{:S(2)}, u32[]{:S(2)}) collective-permute-start(f32[2,16,1,256]{3,2,1,0:T(1,128)S(1)} %pad_maximum_fusion.11), channel_id=1, source_target_pairs={{1,0},{2,1},{3,2},{4,3},{5,4},{6,5},{7,6},{9,8},{10,9},{11,10},{12... | collective-permute-start | bytes 98312 | tf_op jit(solution)/shard_map/while/body/eval_jaxpr/ppermute | solution.py:15
  454.4 8.5 %collective-permute-start = (f32[2,1,16,256]{3,2,1,0:T(8,128)S(1)}, f32[2,1,16,256]{3,2,1,0:T(8,128)S(1)}, u32[]{:S(2)}, u32[]{:S(2)}) collective-permute-start(f32[2,1,16,256]{3,2,1,0:T(8,128)S(1)} %pad_maximum_fusion.10), channel_id=1, source_target_pairs={{8,0},{16,8},{24,16},{9,1},{17,9},{25,17},{10,2},{18,10},{26,18},{... | collective-permute-start | bytes 98312 | tf_op jit(solution)/shard_map/while/body/eval_jaxpr/ppermute | solution.py:15
  466.0 12.4 %collective-permute-start.2 = (f32[2,16,1,256]{3,2,1,0:T(1,128)S(1)}, f32[2,16,1,256]{3,2,1,0:T(1,128)S(1)}, u32[]{:S(2)}, u32[]{:S(2)}) collective-permute-start(f32[2,16,1,256]{3,2,1,0:T(1,128)S(1)} %pad_maximum_fusion.12), channel_id=1, source_target_pairs={{0,1},{1,2},{2,3},{3,4},{4,5},{5,6},{6,7},{8,9},{9,10},{10,11},{11... | collective-permute-start | bytes 98312 | tf_op jit(solution)/shard_map/while/body/eval_jaxpr/ppermute | solution.py:15
  487.4 9.9 %collective-permute-start.1 = (f32[2,16,1,256]{3,2,1,0:T(1,128)S(1)}, f32[2,16,1,256]{3,2,1,0:T(1,128)S(1)}, u32[]{:S(2)}, u32[]{:S(2)}) collective-permute-start(f32[2,16,1,256]{3,2,1,0:T(1,128)S(1)} %pad_maximum_fusion.11), channel_id=1, source_target_pairs={{1,0},{2,1},{3,2},{4,3},{5,4},{6,5},{7,6},{9,8},{10,9},{11,10},{12... | collective-permute-start | bytes 98312 | tf_op jit(solution)/shard_map/while/body/eval_jaxpr/ppermute | solution.py:15
  488.7 8.5 %collective-permute-start = (f32[2,1,16,256]{3,2,1,0:T(8,128)S(1)}, f32[2,1,16,256]{3,2,1,0:T(8,128)S(1)}, u32[]{:S(2)}, u32[]{:S(2)}) collective-permute-start(f32[2,1,16,256]{3,2,1,0:T(8,128)S(1)} %pad_maximum_fusion.10), channel_id=1, source_target_pairs={{8,0},{16,8},{24,16},{9,1},{17,9},{25,17},{10,2},{18,10},{26,18},{... | collective-permute-start | bytes 98312 | tf_op jit(solution)/shard_map/while/body/eval_jaxpr/ppermute | solution.py:15
  500.3 12.4 %collective-permute-start.2 = (f32[2,16,1,256]{3,2,1,0:T(1,128)S(1)}, f32[2,16,1,256]{3,2,1,0:T(1,128)S(1)}, u32[]{:S(2)}, u32[]{:S(2)}) collective-permute-start(f32[2,16,1,256]{3,2,1,0:T(1,128)S(1)} %pad_maximum_fusion.12), channel_id=1, source_target_pairs={{0,1},{1,2},{2,3},{3,4},{4,5},{5,6},{6,7},{8,9},{9,10},{10,11},{11... | collective-permute-start | bytes 98312 | tf_op jit(solution)/shard_map/while/body/eval_jaxpr/ppermute | solution.py:15
  521.7 9.9 %collective-permute-start.1 = (f32[2,16,1,256]{3,2,1,0:T(1,128)S(1)}, f32[2,16,1,256]{3,2,1,0:T(1,128)S(1)}, u32[]{:S(2)}, u32[]{:S(2)}) collective-permute-start(f32[2,16,1,256]{3,2,1,0:T(1,128)S(1)} %pad_maximum_fusion.11), channel_id=1, source_target_pairs={{1,0},{2,1},{3,2},{4,3},{5,4},{6,5},{7,6},{9,8},{10,9},{11,10},{12... | collective-permute-start | bytes 98312 | tf_op jit(solution)/shard_map/while/body/eval_jaxpr/ppermute | solution.py:15
  523.0 8.5 %collective-permute-start = (f32[2,1,16,256]{3,2,1,0:T(8,128)S(1)}, f32[2,1,16,256]{3,2,1,0:T(8,128)S(1)}, u32[]{:S(2)}, u32[]{:S(2)}) collective-permute-start(f32[2,1,16,256]{3,2,1,0:T(8,128)S(1)} %pad_maximum_fusion.10), channel_id=1, source_target_pairs={{8,0},{16,8},{24,16},{9,1},{17,9},{25,17},{10,2},{18,10},{26,18},{... | collective-permute-start | bytes 98312 | tf_op jit(solution)/shard_map/while/body/eval_jaxpr/ppermute | solution.py:15
  534.6 12.4 %collective-permute-start.2 = (f32[2,16,1,256]{3,2,1,0:T(1,128)S(1)}, f32[2,16,1,256]{3,2,1,0:T(1,128)S(1)}, u32[]{:S(2)}, u32[]{:S(2)}) collective-permute-start(f32[2,16,1,256]{3,2,1,0:T(1,128)S(1)} %pad_maximum_fusion.12), channel_id=1, source_target_pairs={{0,1},{1,2},{2,3},{3,4},{4,5},{5,6},{6,7},{8,9},{9,10},{10,11},{11... | collective-permute-start | bytes 98312 | tf_op jit(solution)/shard_map/while/body/eval_jaxpr/ppermute | solution.py:15
  (440 other events, 2458.9 us)
where the time goes:
time: 612 us; the launch traced here: 605 us
  starting transfers between devices  205 us (33%)
  local copies, waits for them, and re-layouts  160 us (26%)
  other arithmetic  119 us (19%)
  matrix products  52.2 us (9%)
  blocking collectives  45.9 us (8%)
  waiting for transfers between devices  13.2 us (2%)
  loops' own time  7.44 us (1%)
    ppermute x64, starting transfers between devices, passed_along(): return lax.ppermute(block, axis, route)  205 us
    slice x96, local copies, waits for them, and re-layouts, difference(): lax.slice_in_dim(values, 1, length, axis=axis)  73.3 us
    sub x48, other arithmetic, turn_parts(): field_h[number] - courant * rotation[number]  50.2 us
    psum x1, blocking collectives, local(): port_power = lax.psum(partial_value, ('gx', 'gy'))  45.9 us
    add x16, other arithmetic, turn_parts(): field_e[1] + factor * rotation[1]  38.7 us
    while x832, local copies, waits for them, and re-layouts  36.9 us
    dot_general x16, matrix products, inject(): lax.dot_general(weighted, depth_table, (((0,), (0,)), ((), ())), precisio...  30.5 us
    dynamic_update_slice x16, local copies, waits for them, and re-layouts, note_power(): return lax.dynamic_update_slice_in_dim(record, drive[None, :], index, 0)  21.4 us
  transfers between devices with their start and end apart: 64, of which 16 were waited for; matrix products, arithmetic and copies ran while one was open for 22% of the time, Pallas kernels for 0%

commit v1 on v0

v1 whole, which is shorter than its diff:
```python
import functools

import jax
import jax.numpy as jnp
from jax import lax
from jax.experimental import pallas as pl
from jax.experimental.pallas import tpu as pltpu
from jax.sharding import PartitionSpec as P

MESH = pl.DeviceIdType.MESH
courant = 0.55
absorb_keep = (0.0, 0.92, 0.75, 0.45)
absorb_take = (0.0, -0.06, -0.18, -0.35)
derivative_pairs = ((2, 1), (1, 2), (0, 2), (2, 0), (1, 0), (0, 1))
UNROLL = 4


def grade_table(grades, table):
    result = jnp.where(grades == 1, table[1], 0.0)
    result = jnp.where(grades == 2, table[2], result)
    return jnp.where(grades == 3, table[3], result)


def split_two(values):
    high = values.astype(jnp.bfloat16)
    low = (values - high.astype(jnp.float32)).astype(jnp.bfloat16)
    return high, low


def kernel(
    e_in, h_in, me_in, mh_in, grades_ref, eps_ref, cell_ref, port_ref, live_ref, inj_ref, wave_ref,
    e_out, h_out, power_ref,
    ef, hf, me, mh, keep, take, factor, source,
    send_e, recv_e, send_h, recv_h, cell_t, cell_f, depth_t, depth, current, record,
    load_sem, store_sem, send_sem, recv_sem,
):
    depth_x, depth_y, depth_z = eps_ref.shape
    ports, slots = inj_ref.shape[1], inj_ref.shape[0]
    steps = wave_ref.shape[0]
    ix, iy = lax.axis_index("gx"), lax.axis_index("gy")
    count_x, count_y = lax.axis_size("gx"), lax.axis_size("gy")
    has_left, has_right = ix > 0, ix < count_x - 1
    has_down, has_up = iy > 0, iy < count_y - 1

    loads = [
        pltpu.make_async_copy(e_in, ef.at[:, pl.ds(0, depth_x)], load_sem.at[0]),
        pltpu.make_async_copy(h_in, hf.at[:, pl.ds(1, depth_x)], load_sem.at[1]),
        pltpu.make_async_copy(me_in, me, load_sem.at[2]),
        pltpu.make_async_copy(mh_in, mh, load_sem.at[3]),
    ]
    for copy in loads:
        copy.start()

    plane = jnp.zeros((depth_y, depth_z), jnp.float32)
    for component in (1, 2):
        ef[component, depth_x] = plane
        hf[component, 0] = plane
    recv_e[...] = jnp.zeros(recv_e.shape, jnp.float32)
    recv_h[...] = jnp.zeros(recv_h.shape, jnp.float32)

    barrier = pltpu.get_barrier_semaphore()
    for present, dx, dy in (
        (has_left, -1, 0), (has_right, 1, 0), (has_down, 0, -1), (has_up, 0, 1)
    ):
        @pl.when(present)
        def _(dx=dx, dy=dy):
            pl.semaphore_signal(
                barrier, inc=1, device_id=(ix + dx, iy + dy), device_id_type=MESH
            )

    cells = (cell_ref[0:1, :] - ix * depth_x) * depth_y + (cell_ref[1:2, :] - iy * depth_y)
    hit = lax.broadcasted_iota(jnp.int32, cell_f.shape, 0) == cells
    cell_f[...] = jnp.where(hit, 1.0, 0.0)
    cell_t[...] = jnp.where(hit, 1.0, 0.0).astype(jnp.bfloat16)
    hit = lax.broadcasted_iota(jnp.int32, depth_t.shape, 0) == cell_ref[2:3, :]
    table = jnp.where(hit, 1.0, 0.0)
    depth_t[...] = table.astype(jnp.bfloat16)
    depth[...] = table.T.astype(jnp.bfloat16)
    live = lax.broadcasted_iota(jnp.int32, (1, slots), 1) < live_ref[0]
    flow = lax.dot_general(
        wave_ref[...], inj_ref[...], (((1,), (1,)), ((), ())), preferred_element_type=jnp.float32
    )
    current[...] = jnp.where(live, flow, 0.0)

    def prepare(x, _):
        for d in range(3):
            level = grades_ref[d, x]
            keep[d, x] = grade_table(level, absorb_keep)
            take[d, x] = grade_table(level, absorb_take)
        factor[x] = courant / eps_ref[x]
        return 0

    lax.fori_loop(0, depth_x, prepare, 0)
    for copy in loads:
        copy.wait()

    def pack_first(x):
        send_e[0, pl.ds(x, 1), :] = ef[0, x, 0:1, :]
        send_e[1, pl.ds(x, 1), :] = ef[2, x, 0:1, :]

    for x in range(depth_x):
        pack_first(x)
    peers = sum(present.astype(jnp.int32) for present in (has_left, has_right, has_down, has_up))
    pl.semaphore_wait(barrier, peers)

    def copies(kind):
        if kind == 0:
            return (
                (has_left, has_right, pltpu.make_async_remote_copy(
                    src_ref=ef.at[pl.ds(1, 2), 0], dst_ref=ef.at[pl.ds(1, 2), depth_x],
                    send_sem=send_sem.at[0], recv_sem=recv_sem.at[0],
                    device_id=(ix - 1, iy), device_id_type=MESH)),
                (has_down, has_up, pltpu.make_async_remote_copy(
                    src_ref=send_e, dst_ref=recv_e,
                    send_sem=send_sem.at[1], recv_sem=recv_sem.at[1],
                    device_id=(ix, iy - 1), device_id_type=MESH)),
            )
        return (
            (has_right, has_left, pltpu.make_async_remote_copy(
                src_ref=hf.at[pl.ds(1, 2), depth_x], dst_ref=hf.at[pl.ds(1, 2), 0],
                send_sem=send_sem.at[2], recv_sem=recv_sem.at[2],
                device_id=(ix + 1, iy), device_id_type=MESH)),
            (has_up, has_down, pltpu.make_async_remote_copy(
                src_ref=send_h, dst_ref=recv_h,
                send_sem=send_sem.at[3], recv_sem=recv_sem.at[3],
                device_id=(ix, iy + 1), device_id_type=MESH)),
        )

    def start(kind):
        for sends, _, copy in copies(kind):
            pl.when(sends)(copy.start)

    def finish(kind):
        for sends, receives, copy in copies(kind):
            pl.when(sends)(copy.wait_send)
            pl.when(receives)(copy.wait_recv)

    rows = lax.broadcasted_iota(jnp.int32, (depth_y, depth_z), 0)
    lanes = lax.broadcasted_iota(jnp.int32, (depth_y, depth_z), 1)

    def curl(x, here, beside, halo, memory, forward):
        turn_y = depth_y - 1 if forward else 1
        turn_z = depth_z - 1 if forward else 1
        edge_y = rows == (depth_y - 1 if forward else 0)
        edge_z = lanes == (depth_z - 1 if forward else 0)
        terms = []
        for number, (component, axis) in enumerate(derivative_pairs):
            value = here[component]
            if axis == 0:
                other = beside[component]
            elif axis == 1:
                line = halo[component // 2, pl.ds(x, 1), :]
                other = jnp.where(edge_y, line, pltpu.roll(value, turn_y, 0))
            else:
                other = jnp.where(edge_z, 0.0, pltpu.roll(value, turn_z, 1))
            slope = other - value if forward else value - other
            carried = keep[axis, x] * memory[number, x] + take[axis, x] * slope
            memory[number, x] = carried
            terms.append(slope + carried)
        return (terms[0] - terms[1], terms[2] - terms[3], terms[4] - terms[5])

    def update_h(block, _):
        for inner in range(UNROLL):
            x = block * UNROLL + inner
            here = [ef[c, x] for c in range(3)]
            beside = [None, ef[1, x + 1], ef[2, x + 1]]
            rotation = curl(x, here, beside, recv_e, me, True)
            fresh = [hf[c, x + 1] - courant * rotation[c] for c in range(3)]
            for c in range(3):
                hf[c, x + 1] = fresh[c]
            send_h[0, pl.ds(x, 1), :] = fresh[0][depth_y - 1:depth_y, :]
            send_h[1, pl.ds(x, 1), :] = fresh[2][depth_y - 1:depth_y, :]
        return 0

    def update_e(block, _):
        for inner in range(UNROLL):
            x = block * UNROLL + inner
            here = [hf[c, x + 1] for c in range(3)]
            beside = [None, hf[1, x], hf[2, x]]
            rotation = curl(x, here, beside, recv_h, mh, False)
            ratio = factor[x]
            fresh = [ef[c, x] + ratio * rotation[c] for c in range(3)]
            fresh[2] = fresh[2] - courant * source[x]
            for c in range(3):
                ef[c, x] = fresh[c]
            send_e[0, pl.ds(x, 1), :] = fresh[0][0:1, :]
            send_e[1, pl.ds(x, 1), :] = fresh[2][0:1, :]
        return 0

    def inject(step):
        high, low = split_two(current[pl.ds(step, 1), :])
        total = None
        for part in (high, low):
            piece = jnp.dot(
                cell_t[...] * part, depth[...], preferred_element_type=jnp.float32
            )
            total = piece if total is None else total + piece
        source[...] = total.reshape(source.shape)

    def read_out(step):
        values = ef[2, pl.ds(0, depth_x)].reshape(depth_x * depth_y, depth_z)
        high, low = split_two(values)
        picked = jnp.dot(high, depth_t[...], preferred_element_type=jnp.float32)
        picked = picked + jnp.dot(low, depth_t[...], preferred_element_type=jnp.float32)
        chosen = jnp.sum(picked * cell_f[...], axis=0, keepdims=True)
        record[pl.ds(step, 1), :] = chosen * current[pl.ds(step, 1), :]

    def turn(step, _):
        start(0)
        inject(step)
        finish(0)
        lax.fori_loop(0, depth_x // UNROLL, update_h, 0)
        start(1)
        read_out((step + steps - 1) % steps)
        finish(1)
        lax.fori_loop(0, depth_x // UNROLL, update_e, 0)
        return 0

    lax.fori_loop(0, steps, turn, 0)
    stores = [
        pltpu.make_async_copy(ef.at[:, pl.ds(0, depth_x)], e_out, store_sem.at[0]),
        pltpu.make_async_copy(hf.at[:, pl.ds(1, depth_x)], h_out, store_sem.at[1]),
    ]
    for copy in stores:
        copy.start()
    read_out(steps - 1)
    member = lax.broadcasted_iota(jnp.int32, (ports, slots), 0) == port_ref[...]
    member = jnp.where(member, 1.0, 0.0).astype(jnp.bfloat16)
    total = None
    for part in split_two(record[...]):
        piece = lax.dot_general(
            part, member, (((1,), (1,)), ((), ())), preferred_element_type=jnp.float32
        )
        total = piece if total is None else total + piece
    power_ref[...] = total
    for copy in stores:
        copy.wait()


def local(
    electric, magnetic, aux_electric, aux_magnetic, grades, permittivity,
    dipole_cell, dipole_port, live_count, injection, waveform,
):
    depth_x, depth_y, depth_z = permittivity.shape
    slots = dipole_cell.shape[1]
    ports, steps = waveform.shape
    block = (depth_x, depth_y, depth_z)
    cells = depth_x * depth_y
    f32 = jnp.float32
    vmem = pl.BlockSpec(memory_space=pltpu.VMEM)
    anywhere = pl.BlockSpec(memory_space=pl.ANY)
    electric, magnetic, power = pl.pallas_call(
        kernel,
        out_shape=(
            jax.ShapeDtypeStruct(electric.shape, f32),
            jax.ShapeDtypeStruct(magnetic.shape, f32),
            jax.ShapeDtypeStruct((steps, ports), f32),
        ),
        in_specs=[anywhere] * 4 + [vmem] * 4
        + [pl.BlockSpec(memory_space=pltpu.SMEM)] + [vmem] * 2,
        out_specs=(anywhere, anywhere, vmem),
        scratch_shapes=[
            pltpu.VMEM((3, depth_x + 1, depth_y, depth_z), f32),
            pltpu.VMEM((3, depth_x + 1, depth_y, depth_z), f32),
            pltpu.VMEM((6,) + block, f32),
            pltpu.VMEM((6,) + block, f32),
            pltpu.VMEM((3,) + block, f32),
            pltpu.VMEM((3,) + block, f32),
            pltpu.VMEM(block, f32),
            pltpu.VMEM(block, f32),
            pltpu.VMEM((2, depth_x, depth_z), f32),
            pltpu.VMEM((2, depth_x, depth_z), f32),
            pltpu.VMEM((2, depth_x, depth_z), f32),
            pltpu.VMEM((2, depth_x, depth_z), f32),
            pltpu.VMEM((cells, slots), jnp.bfloat16),
            pltpu.VMEM((cells, slots), f32),
            pltpu.VMEM((depth_z, slots), jnp.bfloat16),
            pltpu.VMEM((slots, depth_z), jnp.bfloat16),
            pltpu.VMEM((steps, slots), f32),
            pltpu.VMEM((steps, slots), f32),
            pltpu.SemaphoreType.DMA((4,)),
            pltpu.SemaphoreType.DMA((2,)),
            pltpu.SemaphoreType.DMA((4,)),
            pltpu.SemaphoreType.DMA((4,)),
        ],
        compiler_params=pltpu.CompilerParams(
            collective_id=0, has_side_effects=True, vmem_limit_bytes=40 * 1024 * 1024
        ),
    )(
        electric, magnetic, aux_electric, aux_magnetic, grades, permittivity,
        dipole_cell, dipole_port.reshape(1, slots), live_count, injection, waveform.T,
    )
    return electric, magnetic, lax.psum(power, ("gx", "gy"))


def solution(mesh):
    in_specs = (
        P(None, "gx", "gy", None),
        P(None, "gx", "gy", None),
        P(None, "gx", "gy", None),
        P(None, "gx", "gy", None),
        P(None, "gx", "gy", None),
        P("gx", "gy", None),
        P(None, ("gx", "gy")),
        P(("gx", "gy")),
        P(("gx", "gy")),
        P(("gx", "gy"), None),
        P(),
    )
    out_specs = (P(None, "gx", "gy", None), P(None, "gx", "gy", None), P())
    return jax.shard_map(local, mesh=mesh, in_specs=in_specs, out_specs=out_specs, check_vma=False)
```

time: 612 us -> 182 us (0.30); the launches traced: 605 us -> 181 us
  starting transfers between devices: 205 us -> 0 us
  local copies, waits for them, and re-layouts: 160 us -> 12 us
  Pallas kernels: 0 us -> 124 us
  other arithmetic: 119 us -> 0 us
  matrix products: 52.2 us -> 0 us
  waiting for transfers between devices: 13.2 us -> 0 us
  loops' own time: 7.44 us -> 0 us
    ppermute x64 -> x0, starting transfers between devices: 205 us -> none  [passed_along(): return lax.ppermute(block, axis, route)]
    pallas_call x0 -> x1, Pallas kernels: none -> 124 us  [local(): pl.pallas_call(kernel, out_shape=(jax.ShapeDtypeStruct(electric.shape, f3...]
    slice x128 -> x0, local copies, waits for them, and re-layouts: 84.8 us -> none  [the longest x96 73.3 us: difference(): lax.slice_in_dim(values, 1, length, axis=axis)]
    sub x64 -> x0, other arithmetic: 56.9 us -> none  [the longest x48 50.2 us: turn_parts(): field_h[number] - courant * rotation[number]]
    dot_general x34 -> x0, matrix products: 52.2 us -> none  [the longest x16 30.5 us: inject(): lax.dot_general(weighted, depth_table, (((0,), (0,)), ((), ())), precisio...]
    add x34 -> x0, other arithmetic: 45.1 us -> none  [the longest x16 38.7 us: turn_parts(): field_e[1] + factor * rotation[1]]
    while x832 -> x0, local copies, waits for them, and re-layouts: 36.9 us -> none
    dynamic_update_slice x16 -> x0, local copies, waits for them, and re-layouts: 21.4 us -> none  [note_power(): return lax.dynamic_update_slice_in_dim(record, drive[None, :], index, 0)]
  transfers between devices with their start and end apart: 64 -> 0, of which waited for: 16 -> 0; matrix products, arithmetic and copies ran while one was open for 22% -> 0% of each run, Pallas kernels for 0% -> 0%
where the time goes in v1:
time: 182 us; the launch traced here: 181 us
  Pallas kernels  124 us (68%)
  blocking collectives  43.6 us (24%)
  local copies, waits for them, and re-layouts  12 us (7%)
    pallas_call x1, Pallas kernels, local(): pl.pallas_call(kernel, out_shape=(jax.ShapeDtypeStruct(electric.shape, f3...  124 us
    psum x1, blocking collectives, local(): return (electric, magnetic, lax.psum(power, ('gx', 'gy')))  43.6 us
    unnamed x22, local copies, waits for them, and re-layouts  12 us

profile of v1, /device:TPU:0, one launch (start us, length us, event | category | flops | bytes accessed | tf_op | source)
XLA Modules:
  0.0 181.3 jit_solution(7255133204553423496)
XLA Ops:
  1.3 0.0 copy-start
  1.3 1.4 copy-done
  2.7 0.0 copy-start.1
  2.7 1.4 copy-done.1
  4.1 0.0 copy-start.2
  4.1 1.1 copy-done.2
  5.2 0.0 copy-start.3
  5.2 1.1 copy-done.3
  6.4 0.0 copy-start.4
  6.4 1.1 copy-done.4
  7.5 0.0 copy-start.5
  7.5 1.0 copy-done.5
  8.5 0.0 copy-start.6
  8.5 0.9 copy-done.6
  9.5 0.0 copy-start.7
  9.5 0.7 copy-done.7
  10.2 0.0 copy-start.8
  10.2 0.7 copy-done.8
  10.9 0.0 copy-start.9
  10.9 0.7 copy-done.9
  11.6 124.4 %shard_map.130 = (f32[3,16,16,256]{3,2,1,0:T(8,128)S(1)}, f32[3,16,16,256]{3,2,1,0:T(8,128)S(1)}, f32[16,512]{1,0:T(8,128)S(1)}) custom-call(f32[3,16,16,256]{3,2,1,0:T(8,128)S(1)} %copy-done.2, f32[3,16,16,256]{3,2,1,0:T(8,128)S(1)} %copy-done.3, f32[6,16,16,256]{3,2,1,0:T(8,128)S(1)} %copy-done, f32[6,16,16,256]{3,2,1,0:T(8,128)S(1)} %copy-done.1, ...), custom_call_target="tpu_custom_call" | custom-call | tf_op jit(solution)/shard_map/pallas_call | solution.py:252
  136.0 43.6 %psum.7 = f32[16,512]{1,0:T(8,128)} all-reduce(f32[16,512]{1,0:T(8,128)S(1)} %get-tuple-element.8), channel_id=1, replica_groups=mesh['gx'=4,'gy'=8] {'gx','gy'}, use_global_device_ids=true, to_apply=%region_0.0 | all-reduce | flops 8192 | bytes 65536 | tf_op jit(solution)/shard_map/psum | solution.py:293
  179.6 0.9 copy.17
  180.4 0.9 copy.18
Async XLA Ops:
  1.3 1.4 copy-start
  2.7 1.4 copy-start.1
  4.1 1.1 copy-start.2
  5.2 1.1 copy-start.3
  6.4 1.1 copy-start.4
  7.5 1.0 copy-start.5
  8.5 0.9 copy-start.6
  9.5 0.7 copy-start.7
  10.2 0.7 copy-start.8
  10.9 0.7 copy-start.9

commit v2 on v1

--- a/solution.py
+++ b/solution.py
@@ -32,7 +32,8 @@
     e_out, h_out, power_ref,
     ef, hf, me, mh, keep, take, factor, source,
     send_e, recv_e, send_h, recv_h, cell_t, cell_f, depth_t, depth, current, record,
-    load_sem, store_sem, send_sem, recv_sem,
+    share, from_y, from_x, result,
+    load_sem, store_sem, send_sem, recv_sem, send_sum, recv_sum,
 ):
     depth_x, depth_y, depth_z = eps_ref.shape
     ports, slots = inj_ref.shape[1], inj_ref.shape[0]
@@ -59,14 +60,10 @@
     recv_h[...] = jnp.zeros(recv_h.shape, jnp.float32)
 
     barrier = pltpu.get_barrier_semaphore()
-    for present, dx, dy in (
-        (has_left, -1, 0), (has_right, 1, 0), (has_down, 0, -1), (has_up, 0, 1)
-    ):
-        @pl.when(present)
-        def _(dx=dx, dy=dy):
-            pl.semaphore_signal(
-                barrier, inc=1, device_id=(ix + dx, iy + dy), device_id_type=MESH
-            )
+    line_x = [(lax.rem(ix + offset, count_x), iy) for offset in range(1, count_x)]
+    line_y = [(ix, lax.rem(iy + offset, count_y)) for offset in range(1, count_y)]
+    for peer in line_x + line_y:
+        pl.semaphore_signal(barrier, inc=1, device_id=peer, device_id_type=MESH)
 
     cells = (cell_ref[0:1, :] - ix * depth_x) * depth_y + (cell_ref[1:2, :] - iy * depth_y)
     hit = lax.broadcasted_iota(jnp.int32, cell_f.shape, 0) == cells
@@ -100,8 +97,7 @@
 
     for x in range(depth_x):
         pack_first(x)
-    peers = sum(present.astype(jnp.int32) for present in (has_left, has_right, has_down, has_up))
-    pl.semaphore_wait(barrier, peers)
+    pl.semaphore_wait(barrier, len(line_x) + len(line_y))
 
     def copies(kind):
         if kind == 0:
@@ -232,7 +228,38 @@
             part, member, (((1,), (1,)), ((), ())), preferred_element_type=jnp.float32
         )
         total = piece if total is None else total + piece
-    power_ref[...] = total
+    for row in range(steps):
+        share[row] = total[row:row + 1, :]
+    chunk = steps // count_y
+
+    def spread(first, peers, source_of, target):
+        moves = []
+        for number, peer in enumerate(peers):
+            moves.append(pltpu.make_async_remote_copy(
+                src_ref=source_of(peer), dst_ref=target,
+                send_sem=send_sum.at[first + number], recv_sem=recv_sum.at[first + number],
+                device_id=peer, device_id_type=MESH))
+            moves[-1].start()
+        return moves
+
+    def settle(moves):
+        for move in moves:
+            move.wait()
+
+    mine = pl.ds(iy * chunk, chunk)
+    moves = spread(
+        0, line_y, lambda peer: share.at[pl.ds(peer[1] * chunk, chunk)], from_y.at[iy]
+    )
+    from_y[iy] = share[mine]
+    settle(moves)
+    from_x[ix] = sum(from_y[j] for j in range(count_y))
+    first = len(line_y)
+    settle(spread(first, line_x, lambda peer: from_x.at[ix], from_x.at[ix]))
+    result[mine] = sum(from_x[i] for i in range(count_x))
+    first = first + len(line_x)
+    settle(spread(first, line_y, lambda peer: result.at[mine], result.at[mine]))
+    for row in range(steps):
+        power_ref[row:row + 1, :] = result[row]
     for copy in stores:
         copy.wait()
 
@@ -247,8 +274,12 @@
     block = (depth_x, depth_y, depth_z)
     cells = depth_x * depth_y
     f32 = jnp.float32
+    count_x, count_y = lax.axis_size("gx"), lax.axis_size("gy")
+    chunk = steps // count_y
+    assert chunk * count_y == steps
+    transfers = count_x + 2 * count_y
     vmem = pl.BlockSpec(memory_space=pltpu.VMEM)
-    anywhere = pl.BlockSpec(memory_space=pl.ANY)
+    anywhere = pl.BlockSpec(memory_space=pltpu.HBM)
     electric, magnetic, power = pl.pallas_call(
         kernel,
         out_shape=(
@@ -278,19 +309,25 @@
             pltpu.VMEM((slots, depth_z), jnp.bfloat16),
             pltpu.VMEM((steps, slots), f32),
             pltpu.VMEM((steps, slots), f32),
+            pltpu.VMEM((steps, 1, ports), f32),
+            pltpu.VMEM((count_y, chunk, 1, ports), f32),
+            pltpu.VMEM((count_x, chunk, 1, ports), f32),
+            pltpu.VMEM((steps, 1, ports), f32),
             pltpu.SemaphoreType.DMA((4,)),
             pltpu.SemaphoreType.DMA((2,)),
             pltpu.SemaphoreType.DMA((4,)),
             pltpu.SemaphoreType.DMA((4,)),
+            pltpu.SemaphoreType.DMA((transfers,)),
+            pltpu.SemaphoreType.DMA((transfers,)),
         ],
         compiler_params=pltpu.CompilerParams(
-            collective_id=0, has_side_effects=True, vmem_limit_bytes=40 * 1024 * 1024
+            collective_id=0, has_side_effects=True, vmem_limit_bytes=60 * 1024 * 1024
         ),
     )(
         electric, magnetic, aux_electric, aux_magnetic, grades, permittivity,
         dipole_cell, dipole_port.reshape(1, slots), live_count, injection, waveform.T,
     )
-    return electric, magnetic, lax.psum(power, ("gx", "gy"))
+    return electric, magnetic, power
 
 
 def solution(mesh):

time: 182 us -> 149 us (0.82)
  blocking collectives: 43.6 us -> 0 us
  Pallas kernels: 124 us -> 144 us
  local copies, waits for them, and re-layouts: 12 us -> 3.64 us
    psum x1 -> x0, blocking collectives: 43.6 us -> none  [local(): return (electric, magnetic, lax.psum(power, ('gx', 'gy')))]
    pallas_call x1, Pallas kernels: 124 us -> 144 us  [local(): pl.pallas_call(kernel, out_shape=(jax.ShapeDtypeStruct(electric.shape, f3...]
    unnamed x22 -> x7, local copies, waits for them, and re-layouts: 12 us -> 3.64 us
where the time goes in v2:
time: 149 us
  Pallas kernels  144 us (97%)
  local copies, waits for them, and re-layouts  3.64 us (2%)
    pallas_call x1, Pallas kernels, local(): pl.pallas_call(kernel, out_shape=(jax.ShapeDtypeStruct(electric.shape, f3...  144 us
    unnamed x7, local copies, waits for them, and re-layouts  3.64 us

profile of v2, /device:TPU:0, one launch (start us, length us, event | category | flops | bytes accessed | tf_op | source)
XLA Modules:
  0.0 148.9 jit_solution(5779797534357135343)
XLA Ops:
  1.3 143.9 %shard_map.130 = (f32[3,16,16,256]{3,2,1,0:T(8,128)}, f32[3,16,16,256]{3,2,1,0:T(8,128)}, f32[16,512]{1,0:T(8,128)}) custom-call(f32[3,16,16,256]{3,2,1,0:T(8,128)} %e_in.1, f32[3,16,16,256]{3,2,1,0:T(8,128)} %h_in.1, f32[6,16,16,256]{3,2,1,0:T(8,128)} %me_in.1, f32[6,16,16,256]{3,2,1,0:T(8,128)} %mh_in.1, s32[3,16,16,256]{3,2,1,0:T(8,128)} %grades_ref.1, ...), custom_call_target="tpu_custom_call" | custom-call | tf_op jit(solution)/shard_map/pallas_call | solution.py:283
  145.2 0.0 copy-start
  145.2 0.0 copy-start.1
  145.2 2.1 %copy.18 = f32[3,16,16,256]{3,2,1,0:T(8,128)} copy(f32[3,16,16,256]{3,2,1,0:T(8,128)} %get-tuple-element.6) | data formatting | bytes 1572864
  147.4 0.0 copy-done
  147.4 0.9 copy.19
  148.3 0.0 copy-done.1
  148.3 0.6 copy.20
Async XLA Ops:
  145.2 2.2 %copy-start = (f32[3,16,16,256]{3,2,1,0:T(8,128)S(1)}, f32[3,16,16,256]{3,2,1,0:T(8,128)}, u32[]{:S(2)}) copy-start(f32[3,16,16,256]{3,2,1,0:T(8,128)} %get-tuple-element.7) | copy-start | bytes 2359300
  145.2 3.0 %copy-start.1 = (f32[16,512]{1,0:T(8,128)S(1)}, f32[16,512]{1,0:T(8,128)}, u32[]{:S(2)}) copy-start(f32[16,512]{1,0:T(8,128)} %get-tuple-element.8) | copy-start | bytes 98308

commit v3 on v2

--- a/solution.py
+++ b/solution.py
@@ -122,9 +122,9 @@
                 device_id=(ix, iy + 1), device_id_type=MESH)),
         )
 
-    def start(kind):
-        for sends, _, copy in copies(kind):
-            pl.when(sends)(copy.start)
+    def start(kind, side, wanted=True):
+        sends, _, copy = copies(kind)[side]
+        pl.when(jnp.logical_and(sends, wanted))(copy.start)
 
     def finish(kind):
         for sends, receives, copy in copies(kind):
@@ -201,17 +201,26 @@
         chosen = jnp.sum(picked * cell_f[...], axis=0, keepdims=True)
         record[pl.ds(step, 1), :] = chosen * current[pl.ds(step, 1), :]
 
+    blocks = depth_x // UNROLL
+
     def turn(step, _):
-        start(0)
         inject(step)
         finish(0)
-        lax.fori_loop(0, depth_x // UNROLL, update_h, 0)
-        start(1)
+        update_h(blocks - 1, 0)
+        start(1, 0)
+        lax.fori_loop(0, blocks - 1, update_h, 0)
+        start(1, 1)
         read_out((step + steps - 1) % steps)
         finish(1)
-        lax.fori_loop(0, depth_x // UNROLL, update_e, 0)
+        more = step < steps - 1
+        update_e(0, 0)
+        start(0, 0, more)
+        lax.fori_loop(1, blocks, update_e, 0)
+        start(0, 1, more)
         return 0
 
+    start(0, 1)
+    start(0, 0)
     lax.fori_loop(0, steps, turn, 0)
     stores = [
         pltpu.make_async_copy(ef.at[:, pl.ds(0, depth_x)], e_out, store_sem.at[0]),

time: 149 us -> 148 us (level)
  no operation moved by 1% of the time
where the time goes in v3:
time: 148 us
  Pallas kernels  143 us (97%)
  local copies, waits for them, and re-layouts  3.64 us (2%)
    pallas_call x1, Pallas kernels, local(): pl.pallas_call(kernel, out_shape=(jax.ShapeDtypeStruct(electric.shape, f3...  143 us
    unnamed x7, local copies, waits for them, and re-layouts  3.64 us

profile of v3, /device:TPU:0, one launch (start us, length us, event | category | flops | bytes accessed | tf_op | source)
XLA Modules:
  0.0 147.8 jit_solution(13856747401808787073)
XLA Ops:
  1.3 142.9 %shard_map.130 = (f32[3,16,16,256]{3,2,1,0:T(8,128)}, f32[3,16,16,256]{3,2,1,0:T(8,128)}, f32[16,512]{1,0:T(8,128)}) custom-call(f32[3,16,16,256]{3,2,1,0:T(8,128)} %e_in.1, f32[3,16,16,256]{3,2,1,0:T(8,128)} %h_in.1, f32[6,16,16,256]{3,2,1,0:T(8,128)} %me_in.1, f32[6,16,16,256]{3,2,1,0:T(8,128)} %mh_in.1, s32[3,16,16,256]{3,2,1,0:T(8,128)} %grades_ref.1, ...), custom_call_target="tpu_custom_call" | custom-call | tf_op jit(solution)/shard_map/pallas_call | solution.py:292
  144.2 0.0 copy-start
  144.2 0.0 copy-start.1
  144.2 2.1 %copy.18 = f32[3,16,16,256]{3,2,1,0:T(8,128)} copy(f32[3,16,16,256]{3,2,1,0:T(8,128)} %get-tuple-element.6) | data formatting | bytes 1572864
  146.3 0.0 copy-done
  146.3 0.9 copy.19
  147.2 0.0 copy-done.1
  147.2 0.6 copy.20
Async XLA Ops:
  144.2 2.2 %copy-start = (f32[3,16,16,256]{3,2,1,0:T(8,128)S(1)}, f32[3,16,16,256]{3,2,1,0:T(8,128)}, u32[]{:S(2)}) copy-start(f32[3,16,16,256]{3,2,1,0:T(8,128)} %get-tuple-element.7) | copy-start | bytes 2359300
  144.2 3.0 %copy-start.1 = (f32[16,512]{1,0:T(8,128)S(1)}, f32[16,512]{1,0:T(8,128)}, u32[]{:S(2)}) copy-start(f32[16,512]{1,0:T(8,128)} %get-tuple-element.8) | copy-start | bytes 98308
